TPU v7x, 32 devices: a whole 2x2x4 slice. The times are simulated.
32 devices in a mesh: dp: 2 (over y), ctx: 8 (over z, x), segment: 2 (over core).
Axes of the slice: x: 2, y: 2, z: 4, core: 2. Of those that a mesh axis runs over, the one named last changes fastest.
Arguments:
- inputs: bfloat16 [2, 2048, 1536], P('dp', 'ctx'), may hold values from -6 to 6
- cotangent: bfloat16 [2, 2048, 1536], P('dp', 'ctx'), may hold values from -6 to 6
- weights: bfloat16 [2, 1536, 1536], P('segment', 'ctx'), may hold values from -0.15625 to 0.15625
- tap_weights: float32 [2, 3, 1536], P('segment'), may hold values from -3 to 3
- projection: bfloat16 [2, 1536, 256], P('segment'), may hold values from -0.15625 to 0.15625
- dilations: int32 [2], replicated, may hold values from 1 to 64, as said below
Outputs:
- input_grad: bfloat16 [2, 2048, 1536], P('dp', 'ctx', 'segment')
- sketches: float32 [2, 256, 1536], P('segment', 'ctx')
Inputs may be any that keep to these rules, and one draw needn't show every extreme that they name: `dilations`: each entry is a section's dilation; one of the two equals 64.
All inputs are finite; a program needn't handle non-finite values.
Results may differ from a plain program's by a relative error of at most 0.02.
Values may be sent and summed in bfloat16 or wider, within the bound.
A program may use at most 64 MiB of HBM per device.

v0:
```python
import jax
import jax.numpy as jnp
from jax import lax
from jax.sharding import PartitionSpec as P

DMAX = 64


def with_halo(x, sides, width):
    for axis, dim in sides:
        devices, length = (lax.axis_size(axis), x.shape[dim])
        up = [(i, (i + 1) % devices) for i in range(devices - 1)]
        down = [(j, i) for i, j in up]
        last = lax.slice_in_dim(x, length - width, length, axis=dim)
        leading = lax.slice_in_dim(x, 0, width, axis=dim)
        before = lax.ppermute(last, axis, up)
        after = lax.ppermute(leading, axis, down)
        x = jnp.concatenate([before, x, after], axis=dim)
    return x


def passed_along(block, axis, distance):
    devices = range(lax.axis_size(axis))
    route = [(i - distance, i) for i in devices if i - distance in devices]
    return lax.ppermute(block, axis, route)


def activate(values):
    normed = values * lax.rsqrt(jnp.mean(values * values, axis=-1, keepdims=True) + 1e-06)
    return jax.nn.gelu(normed, approximate=True)


def shards(inputs, cotangent, weights, tap_weights, projection, dilations):
    segment_index = lax.axis_index("segment")
    width = inputs.shape[2]
    pair_weights, pair_taps, pair_tests = (weights, tap_weights, projection)
    rows_in = inputs[0]
    grad_out = cotangent[0]
    own_dilation = jnp.where(segment_index == 0, dilations[0], dilations[1])
    late_index = 0
    length = rows_in.shape[0]

    def act_rims(values):
        return with_halo(values, (("ctx", 0),), DMAX)

    def grad_rims(values):
        return with_halo(values, (("ctx", 0),), DMAX)

    full_weights = lax.all_gather(pair_weights, "ctx", axis=1, tiled=True)

    def backward_product(grad, which):
        return lax.dot_general(
            grad, full_weights[which], (((1,), (1,)), ((), ())), preferred_element_type=jnp.float32
        )

    def mix(rows, which, dilation):
        taps = pair_taps[which]
        lower = DMAX - dilation
        upper = DMAX + dilation
        activated = activate(rows.astype(jnp.float32)).astype(jnp.bfloat16)
        padded = act_rims(activated)
        before = lax.dynamic_slice_in_dim(padded, lower, length, 0)
        after = lax.dynamic_slice_in_dim(padded, upper, length, 0)
        mixed = taps[0] * before + taps[1] * activated + taps[2] * after
        return mixed.astype(jnp.bfloat16)

    def backward(rows, mixed, grad, which, dilation):
        taps = pair_taps[which]
        lower = DMAX - dilation
        upper = DMAX + dilation
        grad_mixed = backward_product(grad, which).astype(jnp.bfloat16)
        padded = grad_rims(grad_mixed)
        ahead = lax.dynamic_slice_in_dim(padded, upper, length, 0)
        behind = lax.dynamic_slice_in_dim(padded, lower, length, 0)
        grad_act = taps[0] * ahead + taps[1] * grad_mixed + taps[2] * behind
        primal, pullback = jax.vjp(activate, rows.astype(jnp.float32))
        grad_rows = pullback(grad_act)[0]
        grad_in = (grad.astype(jnp.float32) + grad_rows).astype(jnp.bfloat16)
        sketched = jnp.dot(grad, pair_tests[which], preferred_element_type=jnp.float32).astype(
            jnp.bfloat16
        )
        sketch = lax.dot_general(
            sketched, mixed, (((0,), (0,)), ((), ())), preferred_element_type=jnp.float32
        )
        return (grad_in, sketch)

    first_mixed = mix(rows_in, 0, own_dilation)
    section_out = (
        rows_in.astype(jnp.float32)
        + jnp.dot(first_mixed, full_weights[0], preferred_element_type=jnp.float32)
    ).astype(jnp.bfloat16)
    half = width // 2
    received = passed_along(section_out, "segment", 1)
    late_mixed = mix(received, late_index, own_dilation)
    grad_late, sketch_late = backward(received, late_mixed, grad_out, late_index, own_dilation)
    grad_back = passed_along(grad_late, "segment", -1)
    grad_early, sketch_early = backward(rows_in, first_mixed, grad_back, 0, own_dilation)
    local_sketch = jnp.where(segment_index == 1, sketch_late, sketch_early)
    moved = passed_along(grad_early[:, half:], "segment", 1)
    grad_half = jnp.where(segment_index == 0, grad_early[:, :half], moved)
    summed = lax.psum_scatter(
        local_sketch.astype(jnp.bfloat16), "ctx", scatter_dimension=0, tiled=True
    )
    merged = lax.psum(summed, "dp").astype(jnp.float32)
    return (grad_half[None], merged[None])


def solution(mesh):
    in_specs = (
        P("dp", "ctx", None),
        P("dp", "ctx", None),
        P("segment", "ctx", None),
        P("segment", None, None),
        P("segment", None, None),
        P(),
    )
    out_specs = (P("dp", "ctx", "segment"), P("segment", "ctx", None))
    return jax.shard_map(shards, mesh=mesh, in_specs=in_specs, out_specs=out_specs, check_vma=False)
```

profile of v0, /device:TPU:20, one launch (start us, length us, event | category | flops | bytes accessed | tf_op | source)
XLA Modules:
  0.0 243.1 jit_solution(9777423108458225322)
XLA Ops:
  7.2 0.7 all-gather.2.cloned.1.call-update
  7.9 0.0 reduce-scatter.2.cloned.1.call-start
  8.0 1.4 fusion.52
  9.4 0.6 copy-done.10
  9.9 0.7 fusion.49
  10.6 3.4 %collective-permute-start.2 = (bf16[64,1536]{1,0:T(8,128)(2,1)S(1)}, bf16[64,1536]{1,0:T(8,128)(2,1)S(1)}, u32[]{:S(2)}, u32[]{:S(2)}) collective-permute-start(bf16[64,1536]{1,0:T(8,128)(2,1)S(1)} %get-tuple-element.16), channel_id=1, source_target_pairs={{0,2},{2,4},{4,6},{6,8},{8,10},{10,12},{12,14},{1,3},{3,5},{5,7},{... | collective-permute-start | bytes 589832 | tf_op jit(solution)/shard_map/ppermute | solution.py:16
  14.1 3.3 %collective-permute-start.3 = (bf16[64,1536]{1,0:T(8,128)(2,1)S(1)}, bf16[64,1536]{1,0:T(8,128)(2,1)S(1)}, u32[]{:S(2)}, u32[]{:S(2)}) collective-permute-start(bf16[64,1536]{1,0:T(8,128)(2,1)S(1)} %get-tuple-element.17), channel_id=1, source_target_pairs={{2,0},{4,2},{6,4},{8,6},{10,8},{12,10},{14,12},{3,1},{5,3},{7,5},{... | collective-permute-start | bytes 589832 | tf_op jit(solution)/shard_map/ppermute | solution.py:17
  17.4 0.6 fusion.77
  19.3 0.1 slice_reduce_fusion.2
  19.4 0.8 collective-permute-done.2
  20.2 6.4 %collective-permute-done.3 = bf16[64,1536]{1,0:T(8,128)(2,1)S(1)} collective-permute-done((bf16[64,1536]{1,0:T(8,128)(2,1)S(1)}, bf16[64,1536]{1,0:T(8,128)(2,1)S(1)}, u32[]{:S(2)}, u32[]{:S(2)}) %collective-permute-start.3) | collective-permute-done | bytes 196640 | tf_op jit(solution)/shard_map/ppermute | solution.py:17
  26.6 0.1 pad_maximum_fusion.1
  26.7 1.2 add_convert_fusion.1
  27.9 62.0 %all-gather.2.cloned.1.call-done = bf16[1,1536,1536]{2,1,0:T(8,128)(2,1)} async-done(((bf16[1,192,1536]{2,1,0:T(8,128)(2,1)}), bf16[1,1536,1536]{2,1,0:T(8,128)(2,1)}) %all-gather.2.cloned.1.call-update) | async-done | bytes 4718608 | tf_op jit(solution)/shard_map/all_gather | solution.py:49
  89.9 3.9 %fusion.19 = bf16[256,1536]{1,0:T(8,128)(2,1)S(1)} fusion(bf16[256,1536]{1,0:T(8,128)(2,1)S(1)} %add_convert_fusion.1, bf16[1,1536,1536]{2,1,0:T(8,128)(2,1)} %all-gather.2.cloned.1.call-done, bf16[1,256,1536]{2,1,0:T(8,128)(2,1)S(1)} %copy-done.1), kind=kOutput, calls=%fused_computation.27 | convolution fusion | flops 1209139200 | bytes 7077888 | tf_op jit(solution)/shard_map/dot_general | solution.py:90
  93.8 1.3 collective-permute-start.4
  95.2 1.4 fusion.22
  96.6 2.5 %collective-permute-start = (bf16[64,1536]{1,0:T(8,128)(2,1)S(1)}, bf16[64,1536]{1,0:T(8,128)(2,1)S(1)}, u32[]{:S(2)}, u32[]{:S(2)}) collective-permute-start(bf16[64,1536]{1,0:T(8,128)(2,1)S(1)} %get-tuple-element.14), channel_id=1, source_target_pairs={{0,2},{2,4},{4,6},{6,8},{8,10},{10,12},{12,14},{1,3},{3,5},{5,7},{... | collective-permute-start | bytes 589832 | tf_op jit(solution)/shard_map/ppermute | solution.py:16
  99.1 4.3 %collective-permute-start.1 = (bf16[64,1536]{1,0:T(8,128)(2,1)S(1)}, bf16[64,1536]{1,0:T(8,128)(2,1)S(1)}, u32[]{:S(2)}, u32[]{:S(2)}) collective-permute-start(bf16[64,1536]{1,0:T(8,128)(2,1)S(1)} %get-tuple-element.15), channel_id=1, source_target_pairs={{2,0},{4,2},{6,4},{8,6},{10,8},{12,10},{14,12},{3,1},{5,3},{7,5},{... | collective-permute-start | bytes 589832 | tf_op jit(solution)/shard_map/ppermute | solution.py:17
  103.4 1.7 collective-permute-done
  105.1 4.1 %collective-permute-done.1 = bf16[64,1536]{1,0:T(8,128)(2,1)S(1)} collective-permute-done((bf16[64,1536]{1,0:T(8,128)(2,1)S(1)}, bf16[64,1536]{1,0:T(8,128)(2,1)S(1)}, u32[]{:S(2)}, u32[]{:S(2)}) %collective-permute-start.1) | collective-permute-done | bytes 196640 | tf_op jit(solution)/shard_map/ppermute | solution.py:17
  109.2 0.1 pad_maximum_fusion
  109.3 0.2 fusion.44
  109.6 2.5 %fusion.45 = (f32[256]{0:T(256)S(1)}, f32[256,1536]{1,0:T(8,128)S(1)}, bf16[256,1536]{1,0:T(8,128)(2,1)S(1)}) fusion(bf16[256,1536]{1,0:T(8,128)(2,1)S(1)} %collective-permute-done.4, f32[256]{0:T(256)S(1)} %fusion.70, bf16[384,1536]{1,0:T(8,128)(2,1)S(1)} %pad_maximum_fusion, s32[]{:T(128)S(6)} %select_n.35, f32[1536]{0:T(1024)S(1)} %get-tuple-element.3, ...), kind=kLoop, calls=%fused_computation.49 | loop fusion | flops 12975872 | bytes 5525512 | tf_op jit(solution)/shard_map/transpose(jvp())/reduce_sum | solution.py:29
  112.1 1.4 fusion.35
  113.5 1.3 collective-permute-start.5
  114.7 0.8 fusion.73
  115.5 2.3 collective-permute-start.9
  117.9 4.4 %collective-permute-start.10 = (bf16[64,1536]{1,0:T(8,128)(2,1)}, bf16[64,1536]{1,0:T(8,128)(2,1)S(1)}, u32[]{:S(2)}, u32[]{:S(2)}) collective-permute-start(bf16[64,1536]{1,0:T(8,128)(2,1)} %get-tuple-element.11), channel_id=1, source_target_pairs={{2,0},{4,2},{6,4},{8,6},{10,8},{12,10},{14,12},{3,1},{5,3},{7,5},{... | collective-permute-start | bytes 589832 | tf_op jit(solution)/shard_map/ppermute | solution.py:17
  122.3 3.9 %collective-permute-done.9 = bf16[64,1536]{1,0:T(8,128)(2,1)S(1)} collective-permute-done((bf16[64,1536]{1,0:T(8,128)(2,1)}, bf16[64,1536]{1,0:T(8,128)(2,1)S(1)}, u32[]{:S(2)}, u32[]{:S(2)}) %collective-permute-start.9) | collective-permute-done | bytes 196640 | tf_op jit(solution)/shard_map/ppermute | solution.py:16
  126.2 4.3 %collective-permute-done.10 = bf16[64,1536]{1,0:T(8,128)(2,1)S(1)} collective-permute-done((bf16[64,1536]{1,0:T(8,128)(2,1)}, bf16[64,1536]{1,0:T(8,128)(2,1)S(1)}, u32[]{:S(2)}, u32[]{:S(2)}) %collective-permute-start.10) | collective-permute-done | bytes 196640 | tf_op jit(solution)/shard_map/ppermute | solution.py:17
  130.5 1.1 pad_maximum_fusion.3
  131.6 3.9 %fusion.54 = bf16[256,1536]{1,0:T(8,128)(2,1)} fusion(bf16[256,1536]{1,0:T(8,128)(2,1)S(1)} %get-tuple-element.9, bf16[1,1536,256]{2,1,0:T(8,128)(2,1)S(1)} %copy-done, bf16[1,256,1536]{2,1,0:T(8,128)(2,1)} %param.7, bf16[384,1536]{1,0:T(8,128)(2,1)} %pad_maximum_fusion.3, s32[]{:T(128)S(6)} %select_n.34, s32[]{:T(128)S(6)} %select_n.35, ...), kind=kOutput, calls=%fused_computation.66 | convolution fusion | flops 406257664 | bytes 4739080 | tf_op jit(solution)/shard_map/dot_general | solution.py:82
  135.5 3.7 %fusion.25 = bf16[256,1536]{1,0:T(8,128)(2,1)S(1)} fusion(bf16[256,1536]{1,0:T(8,128)(2,1)S(1)} %collective-permute-done.5, bf16[1,1536,1536]{2,1,0:T(8,128)(2,1)} %all-gather.2.cloned.1.call-done), kind=kOutput, calls=%fused_computation.29 | convolution fusion | flops 1208352768 | bytes 6291456 | tf_op jit(solution)/shard_map/dot_general | solution.py:52
  139.3 0.8 fusion.74
  140.0 2.6 %collective-permute-start.6 = (bf16[64,1536]{1,0:T(8,128)(2,1)}, bf16[64,1536]{1,0:T(8,128)(2,1)S(1)}, u32[]{:S(2)}, u32[]{:S(2)}) collective-permute-start(bf16[64,1536]{1,0:T(8,128)(2,1)} %get-tuple-element.12), channel_id=1, source_target_pairs={{0,2},{2,4},{4,6},{6,8},{8,10},{10,12},{12,14},{1,3},{3,5},{5,7},{... | collective-permute-start | bytes 589832 | tf_op jit(solution)/shard_map/ppermute | solution.py:16
  142.6 4.2 %collective-permute-start.7 = (bf16[64,1536]{1,0:T(8,128)(2,1)}, bf16[64,1536]{1,0:T(8,128)(2,1)S(1)}, u32[]{:S(2)}, u32[]{:S(2)}) collective-permute-start(bf16[64,1536]{1,0:T(8,128)(2,1)} %get-tuple-element.13), channel_id=1, source_target_pairs={{2,0},{4,2},{6,4},{8,6},{10,8},{12,10},{14,12},{3,1},{5,3},{7,5},{... | collective-permute-start | bytes 589832 | tf_op jit(solution)/shard_map/ppermute | solution.py:17
  146.8 3.2 %fusion.18 = bf16[256,1536]{1,0:T(8,128)(2,1)} fusion(bf16[256,1536]{1,0:T(8,128)(2,1)} %fusion.54, bf16[256,1536]{1,0:T(8,128)(2,1)} %copy-done.2, bf16[256,1536]{1,0:T(8,128)(2,1)S(1)} %collective-permute-done.5, bf16[1,1536,256]{2,1,0:T(8,128)(2,1)S(1)} %copy-done, pred[]{:T(512)S(6)} %eq.8), kind=kOutput, calls=%fused_computation.26 | convolution fusion | flops 403111936 | bytes 3932161 | tf_op jit(solution)/shard_map/dot_general | solution.py:82
  150.0 0.2 all-reduce.2.cloned.1.call-start
  150.2 3.9 %collective-permute-done.7 = bf16[64,1536]{1,0:T(8,128)(2,1)S(1)} collective-permute-done((bf16[64,1536]{1,0:T(8,128)(2,1)}, bf16[64,1536]{1,0:T(8,128)(2,1)S(1)}, u32[]{:S(2)}, u32[]{:S(2)}) %collective-permute-start.7) | collective-permute-done | bytes 196640 | tf_op jit(solution)/shard_map/ppermute | solution.py:17
  154.2 0.1 pad_maximum_fusion.2
  154.3 2.4 fusion.53
  156.7 0.5 fusion.37
  157.1 2.0 collective-permute-start.8
  159.1 53.4 %reduce-scatter.2.cloned.1.call-done = bf16[32,1536]{1,0:T(8,128)(2,1)} async-done(((bf16[256,1536]{1,0:T(8,128)(2,1)}), bf16[32,1536]{1,0:T(8,128)(2,1)}) %reduce-scatter.2.cloned.1.call-update) | async-done | bytes 98320 | tf_op jit(solution)/shard_map/reduce_scatter | solution.py:101
  212.5 0.8 fusion.67
  213.3 21.7 %all-reduce.2.cloned.1.call-done = bf16[1,32,1536]{2,1,0:T(8,128)(2,1)} async-done(((bf16[1,32,1536]{2,1,0:T(8,128)(2,1)}), bf16[1,32,1536]{2,1,0:T(8,128)(2,1)}) %all-reduce.2.cloned.1.call-update) | async-done | bytes 98320 | tf_op jit(solution)/shard_map/psum | solution.py:104
  235.0 1.6 broadcast_in_dim.23
  (41 shorter events, 0.3 us)
Async XLA Ops:
  7.2 124.4 %copy-start = (bf16[1,1536,256]{2,1,0:T(8,128)(2,1)S(1)}, bf16[1,1536,256]{2,1,0:T(8,128)(2,1)}, u32[]{:S(2)}) copy-start(bf16[1,1536,256]{2,1,0:T(8,128)(2,1)} %param.10) | copy-start | bytes 2359300
  7.2 2.8 %copy-start.1 = (bf16[1,256,1536]{2,1,0:T(8,128)(2,1)S(1)}, bf16[1,256,1536]{2,1,0:T(8,128)(2,1)}, u32[]{:S(2)}) copy-start(bf16[1,256,1536]{2,1,0:T(8,128)(2,1)} %param.6) | copy-start | bytes 2359300
  7.2 82.7 %all-gather.2.cloned.1.call-start = ((), (), s32[]{:S(2)}) async-start(), calls=%async_computation.1 | async-start | bytes 5308416 | tf_op jit(solution)/shard_map/all_gather | solution.py:49
  7.9 9.5 %copy-start.12 = (s32[2]{0:T(128)S(1)}, s32[2]{0:T(128)}, u32[]{:S(2)}) copy-start(s32[2]{0:T(128)} %param.11) | copy-start | bytes 28
  7.9 11.4 %copy-start.9 = (f32[1,3,1536]{2,0,1:T(1,128)S(1)}, f32[1,3,1536]{2,0,1:T(1,128)}, u32[]{:S(2)}) copy-start(f32[1,3,1536]{2,0,1:T(1,128)} %param.9) | copy-start | bytes 55300
  7.9 204.5 %reduce-scatter.2.cloned.1.call-start = ((), (), s32[]{:S(2)}) async-start(), calls=%async_computation.2 | async-start | bytes 884736 | tf_op jit(solution)/shard_map/reduce_scatter | solution.py:101
  9.4 0.6 copy-start.10
  9.9 16.8 %copy-start.7 = (f32[256]{0:T(256)}, f32[256]{0:T(256)S(1)}, u32[]{:S(2)}) copy-start(f32[256]{0:T(256)S(1)} %fusion.69) | copy-start | bytes 3076
  10.6 9.5 %collective-permute-start.2 = (bf16[64,1536]{1,0:T(8,128)(2,1)S(1)}, bf16[64,1536]{1,0:T(8,128)(2,1)S(1)}, u32[]{:S(2)}, u32[]{:S(2)}) collective-permute-start(bf16[64,1536]{1,0:T(8,128)(2,1)S(1)} %get-tuple-element.16), channel_id=1, source_target_pairs={{0,2},{2,4},{4,6},{6,8},{8,10},{10,12},{12,14},{1,3},{3,5},{5,7},{... | collective-permute-start | bytes 589832 | tf_op jit(solution)/shard_map/ppermute | solution.py:16
  14.1 12.6 %collective-permute-start.3 = (bf16[64,1536]{1,0:T(8,128)(2,1)S(1)}, bf16[64,1536]{1,0:T(8,128)(2,1)S(1)}, u32[]{:S(2)}, u32[]{:S(2)}) collective-permute-start(bf16[64,1536]{1,0:T(8,128)(2,1)S(1)} %get-tuple-element.17), channel_id=1, source_target_pairs={{2,0},{4,2},{6,4},{8,6},{10,8},{12,10},{14,12},{3,1},{5,3},{7,5},{... | collective-permute-start | bytes 589832 | tf_op jit(solution)/shard_map/ppermute | solution.py:17
  19.4 90.2 %copy-start.5 = (f32[1536]{0:T(1024)}, f32[1536]{0:T(1024)S(1)}, u32[]{:S(2)}) copy-start(f32[1536]{0:T(1024)S(1)} %get-tuple-element.4) | copy-start | bytes 18436
  27.9 65.9 %copy-start.2 = (bf16[256,1536]{1,0:T(8,128)(2,1)}, bf16[256,1536]{1,0:T(8,128)(2,1)S(1)}, u32[]{:S(2)}) copy-start(bf16[256,1536]{1,0:T(8,128)(2,1)S(1)} %add_convert_fusion.1) | copy-start | bytes 2359300
  27.9 67.3 %copy-start.3 = (bf16[1,256,1536]{2,1,0:T(8,128)(2,1)S(1)}, bf16[1,256,1536]{2,1,0:T(8,128)(2,1)}, u32[]{:S(2)}) copy-start(bf16[1,256,1536]{2,1,0:T(8,128)(2,1)} %param.7) | copy-start | bytes 2359300
  89.9 5.2 %copy-start.13 = (bf16[1,1536,1536]{2,1,0:T(8,128)(2,1)S(1)}, bf16[1,1536,1536]{2,1,0:T(8,128)(2,1)}, u32[]{:S(2)}) copy-start(bf16[1,1536,1536]{2,1,0:T(8,128)(2,1)} %all-gather.2.cloned.1.call-done) | copy-start | bytes 14155780
  93.8 15.5 %collective-permute-start.4 = (bf16[256,1536]{1,0:T(8,128)(2,1)S(1)}, bf16[256,1536]{1,0:T(8,128)(2,1)S(1)}, u32[]{:S(2)}, u32[]{:S(2)}) collective-permute-start(bf16[256,1536]{1,0:T(8,128)(2,1)S(1)} %fusion.19), channel_id=1, source_target_pairs={{0,1},{2,3},{4,5},{6,7},{8,9},{10,11},{12,13},{14,15},{16,17},{18,... | collective-permute-start | bytes 2359304 | tf_op jit(solution)/shard_map/ppermute | solution.py:25
  96.6 8.5 %collective-permute-start = (bf16[64,1536]{1,0:T(8,128)(2,1)S(1)}, bf16[64,1536]{1,0:T(8,128)(2,1)S(1)}, u32[]{:S(2)}, u32[]{:S(2)}) collective-permute-start(bf16[64,1536]{1,0:T(8,128)(2,1)S(1)} %get-tuple-element.14), channel_id=1, source_target_pairs={{0,2},{2,4},{4,6},{6,8},{8,10},{10,12},{12,14},{1,3},{3,5},{5,7},{... | collective-permute-start | bytes 589832 | tf_op jit(solution)/shard_map/ppermute | solution.py:16
  99.1 10.1 %collective-permute-start.1 = (bf16[64,1536]{1,0:T(8,128)(2,1)S(1)}, bf16[64,1536]{1,0:T(8,128)(2,1)S(1)}, u32[]{:S(2)}, u32[]{:S(2)}) collective-permute-start(bf16[64,1536]{1,0:T(8,128)(2,1)S(1)} %get-tuple-element.15), channel_id=1, source_target_pairs={{2,0},{4,2},{6,4},{8,6},{10,8},{12,10},{14,12},{3,1},{5,3},{7,5},{... | collective-permute-start | bytes 589832 | tf_op jit(solution)/shard_map/ppermute | solution.py:17
  109.6 2.5 %copy-start.4 = (bf16[1,256,1536]{2,1,0:T(8,128)(2,1)S(1)}, bf16[1,256,1536]{2,1,0:T(8,128)(2,1)}, u32[]{:S(2)}) copy-start(bf16[1,256,1536]{2,1,0:T(8,128)(2,1)} %param.7) | copy-start | bytes 2359300
  113.5 22.0 %collective-permute-start.5 = (bf16[256,1536]{1,0:T(8,128)(2,1)}, bf16[256,1536]{1,0:T(8,128)(2,1)S(1)}, u32[]{:S(2)}, u32[]{:S(2)}) collective-permute-start(bf16[256,1536]{1,0:T(8,128)(2,1)} %fusion.35), channel_id=1, source_target_pairs={{1,0},{3,2},{5,4},{7,6},{9,8},{11,10},{13,12},{15,14},{17,16},{19,... | collective-permute-start | bytes 2359304 | tf_op jit(solution)/shard_map/ppermute | solution.py:25
  115.5 10.7 %collective-permute-start.9 = (bf16[64,1536]{1,0:T(8,128)(2,1)}, bf16[64,1536]{1,0:T(8,128)(2,1)S(1)}, u32[]{:S(2)}, u32[]{:S(2)}) collective-permute-start(bf16[64,1536]{1,0:T(8,128)(2,1)} %get-tuple-element.10), channel_id=1, source_target_pairs={{0,2},{2,4},{4,6},{6,8},{8,10},{10,12},{12,14},{1,3},{3,5},{5,7},{... | collective-permute-start | bytes 589832 | tf_op jit(solution)/shard_map/ppermute | solution.py:16
  117.9 12.6 %collective-permute-start.10 = (bf16[64,1536]{1,0:T(8,128)(2,1)}, bf16[64,1536]{1,0:T(8,128)(2,1)S(1)}, u32[]{:S(2)}, u32[]{:S(2)}) collective-permute-start(bf16[64,1536]{1,0:T(8,128)(2,1)} %get-tuple-element.11), channel_id=1, source_target_pairs={{2,0},{4,2},{6,4},{8,6},{10,8},{12,10},{14,12},{3,1},{5,3},{7,5},{... | collective-permute-start | bytes 589832 | tf_op jit(solution)/shard_map/ppermute | solution.py:17
  140.0 10.2 %collective-permute-start.6 = (bf16[64,1536]{1,0:T(8,128)(2,1)}, bf16[64,1536]{1,0:T(8,128)(2,1)S(1)}, u32[]{:S(2)}, u32[]{:S(2)}) collective-permute-start(bf16[64,1536]{1,0:T(8,128)(2,1)} %get-tuple-element.12), channel_id=1, source_target_pairs={{0,2},{2,4},{4,6},{6,8},{8,10},{10,12},{12,14},{1,3},{3,5},{5,7},{... | collective-permute-start | bytes 589832 | tf_op jit(solution)/shard_map/ppermute | solution.py:16
  142.6 11.6 %collective-permute-start.7 = (bf16[64,1536]{1,0:T(8,128)(2,1)}, bf16[64,1536]{1,0:T(8,128)(2,1)S(1)}, u32[]{:S(2)}, u32[]{:S(2)}) collective-permute-start(bf16[64,1536]{1,0:T(8,128)(2,1)} %get-tuple-element.13), channel_id=1, source_target_pairs={{2,0},{4,2},{6,4},{8,6},{10,8},{12,10},{14,12},{3,1},{5,3},{7,5},{... | collective-permute-start | bytes 589832 | tf_op jit(solution)/shard_map/ppermute | solution.py:17
  150.0 85.1 %all-reduce.2.cloned.1.call-start = ((), (), s32[]{:S(2)}) async-start(), calls=%async_computation.3 | async-start | bytes 196608 | tf_op jit(solution)/shard_map/psum | solution.py:104
  150.2 4.0 %copy-start.6 = (f32[1536]{0:T(1024)S(1)}, f32[1536]{0:T(1024)}, u32[]{:S(2)}) copy-start(f32[1536]{0:T(1024)} %copy-done.5) | copy-start | bytes 18436
  150.2 4.0 %copy-start.8 = (f32[256]{0:T(256)S(1)}, f32[256]{0:T(256)}, u32[]{:S(2)}) copy-start(f32[256]{0:T(256)} %copy-done.7) | copy-start | bytes 3076
  154.3 2.4 copy-start.11
  157.1 55.3 %collective-permute-start.8 = (bf16[256,768]{1,0:T(8,128)(2,1)S(1)}, bf16[256,768]{1,0:T(8,128)(2,1)S(1)}, u32[]{:S(2)}, u32[]{:S(2)}) collective-permute-start(bf16[256,768]{1,0:T(8,128)(2,1)S(1)} %slice.79), channel_id=1, source_target_pairs={{0,1},{2,3},{4,5},{6,7},{8,9},{10,11},{12,13},{14,15},{16,17},{18,... | collective-permute-start | bytes 1179656 | tf_op jit(solution)/shard_map/ppermute | solution.py:25
Sparse Core Ops, SparseCore 0:
  10.2 79.7 all-gather.1
  150.1 62.3 reduce-scatter.1
  214.7 20.2 all-reduce.1
where the time goes:
time: 246 us; the launch traced here: 243 us
  waiting for transfers between devices  163 us (66%)
  starting transfers between devices  31.8 us (13%)
  matrix products  16.1 us (7%)
  between operations  15.5 us (6%)
  other arithmetic  13.9 us (6%)
  local copies, waits for them, and re-layouts  2.89 us (1%)
    all_gather x1, waiting for transfers between devices, shards(): full_weights = lax.all_gather(pair_weights, 'ctx', axis=1, tiled=True)  62 us
    reduce_scatter x1, waiting for transfers between devices, shards(): lax.psum_scatter(local_sketch.astype(jnp.bfloat16), 'ctx', scatter_dimens...  53.4 us
    psum x1, waiting for transfers between devices, shards(): merged = lax.psum(summed, 'dp').astype(jnp.float32)  21.7 us
    ppermute x4, waiting for transfers between devices, with_halo(): after = lax.ppermute(leading, axis, down)  18.8 us
    ppermute x4, starting transfers between devices, with_halo(): after = lax.ppermute(leading, axis, down)  16.2 us
    ppermute x4, starting transfers between devices, with_halo(): before = lax.ppermute(last, axis, up)  10.8 us
    dot_general x2, matrix products, backward(): lax.dot_general(sketched, mixed, (((0,), (0,)), ((), ())), preferred_elem...  7.09 us
    ppermute x4, waiting for transfers between devices, with_halo(): before = lax.ppermute(last, axis, up)  6.41 us
  transfers between devices with their start and end apart: 14, of which 10 were waited for; matrix products, arithmetic and copies ran while one was open for 7% of the time, Pallas kernels for 0%

commit v1 on v0

v1 whole, which is shorter than its diff:
```python
import functools

import jax
import jax.numpy as jnp
from jax import lax
from jax.experimental import pallas as pl
from jax.experimental.pallas import tpu as pltpu
from jax.sharding import PartitionSpec as P

DMAX = 64
MESH = pl.DeviceIdType.MESH
F32 = jnp.float32
BF16 = jnp.bfloat16
ROOT = 0.7978845608028654
CUBIC = 0.044715


def line_width(n):
    width = 1
    while 4 * width * width <= n:
        width *= 2
    return width


def kernel(
    n, m, x_ref, g_ref, w_ref, tap_ref, proj_ref, dil_ref, out_ref, sk_ref,
    wf, act, halo_a, halo_g, mixed, gu, ga, first, second, other, sk, rs, dpb, pb,
    w_send, w_recv, h_send, h_recv, c_send, c_recv, rs_send, rs_recv, dp_send, dp_recv,
):
    me = lax.axis_index("ctx")
    dp = lax.axis_index("dp")
    seg = lax.axis_index("segment")
    length, width = x_ref.shape
    rows = w_ref.shape[0]
    kr = sk.shape[1]
    X = line_width(n)
    Z = n // X
    z = me // X
    x = lax.rem(me, X)
    crossing = m % 2 == 0 and rows % 48 == 0
    parts = 2 if crossing else 1
    pr = rows // 3 if crossing else rows
    q = lax.rem(dp, 2) if crossing else 0

    barrier = pltpu.get_barrier_semaphore()
    for k in range(1, n):
        pl.semaphore_signal(barrier, inc=1, device_id={"ctx": lax.rem(me + k, n)}, device_id_type=MESH)
    for k in range(1, m):
        pl.semaphore_signal(barrier, inc=1, device_id={"dp": lax.rem(dp + k, m)}, device_id_type=MESH)
    pl.semaphore_signal(barrier, inc=1, device_id={"segment": 1 - seg}, device_id_type=MESH)
    pl.semaphore_wait(barrier, n + m - 1)

    def piece(block, part):
        return pl.ds(pl.multiple_of(block * rows + part * pr, 16), pr)

    def w_copy(block, part, direction, where, own=False):
        src = w_ref.at[pl.ds(pl.multiple_of(part * pr, 16), pr)] if own else wf.at[piece(block, part)]
        return pltpu.make_async_remote_copy(
            src_ref=src,
            dst_ref=wf.at[piece(block, part)],
            send_sem=w_send.at[block, part, direction],
            recv_sem=w_recv.at[block, part],
            device_id=where,
            device_id_type=MESH,
        )

    def sends_z(block, part, up, own=False):
        if up:
            return (z < Z - 1, lambda: w_copy(block, part, 0, {"ctx": me + X}, own))
        return (z > 0, lambda: w_copy(block, part, 1, {"ctx": me - X}, own))

    def sends_x(block, part, right, own=False):
        if right:
            return (x < X - 1, lambda: w_copy(block, part, 2, {"ctx": me + 1}, own))
        return (x > 0, lambda: w_copy(block, part, 3, {"ctx": me - 1}, own))

    pending = []

    def issue(guard, entry):
        cond, make = entry
        if guard is not None:
            cond = jnp.logical_and(guard, cond)

        @pl.when(cond)
        def _():
            make().start()

        pending.append((cond, make))

    def cross(guard, block, part):
        if crossing:
            cond = part == 2 * q
            if guard is not None:
                cond = jnp.logical_and(guard, cond)
            make = lambda: w_copy(block, part, 4, {"dp": dp + 1 - 2 * q})

            @pl.when(cond)
            def _():
                make().start()

            pending.append((cond, make))

    def arrived(guard, block, part):
        @pl.when(guard)
        def _():
            w_copy(block, part, 0, {"ctx": me}).wait_recv()

    def start_weights():
        for j in range(parts):
            for entry in (
                sends_z(me, q + j, True, True),
                sends_z(me, q + j, False, True),
                sends_x(me, q + j, True, True),
                sends_x(me, q + j, False, True),
            ):
                issue(None, entry)

    def spread_x(step):
        for t in range(1, X):
            for j in range(parts):
                part = q + j
                for sign in (-1, 1):
                    for side in ((0,) if step == 0 else (-1, 1)):
                        zz = z + side * step
                        xx = x + sign * t
                        guard = functools.reduce(
                            jnp.logical_and, [zz >= 0, zz < Z, xx >= 0, xx < X]
                        )
                        block = jnp.clip(zz, 0, Z - 1) * X + jnp.clip(xx, 0, X - 1)
                        arrived(guard, block, part)
                        if t < X - 1:
                            issue(guard, sends_x(block, part, sign < 0))
                        cross(guard, block, part)

    def gather_weights():
        for step in range(1, Z):
            for j in range(parts):
                part = q + j
                for up in (True, False):
                    zz = z - step if up else z + step
                    guard = zz >= 0 if up else zz < Z
                    block = jnp.clip(zz, 0, Z - 1) * X + x
                    arrived(guard, block, part)
                    if step < Z - 1:
                        issue(guard, sends_z(block, part, up))
                    issue(guard, sends_x(block, part, True))
                    issue(guard, sends_x(block, part, False))
                    cross(guard, block, part)
            spread_x(step - 1)
        spread_x(Z - 1)
        if crossing:
            for k in range(1, n):
                block = lax.rem(me + k, n)
                w_copy(block, 2 - 2 * q, 4, {"dp": dp}).wait_recv()

    def halo_copies(which, src, dst):
        down = pltpu.make_async_remote_copy(
            src_ref=src.at[pl.ds(0, DMAX)], dst_ref=dst.at[pl.ds(DMAX, DMAX)],
            send_sem=h_send.at[which, 0], recv_sem=h_recv.at[which, 1],
            device_id={"ctx": me - 1}, device_id_type=MESH,
        )
        up = pltpu.make_async_remote_copy(
            src_ref=src.at[pl.ds(length - DMAX, DMAX)], dst_ref=dst.at[pl.ds(0, DMAX)],
            send_sem=h_send.at[which, 1], recv_sem=h_recv.at[which, 0],
            device_id={"ctx": me + 1}, device_id_type=MESH,
        )
        return down, up

    def start_halo(which, src, dst):
        down, up = halo_copies(which, src, dst)

        @pl.when(me > 0)
        def _():
            down.start()

        @pl.when(me == 0)
        def _():
            dst[pl.ds(0, DMAX), :] = jnp.zeros((DMAX, width), BF16)

        @pl.when(me < n - 1)
        def _():
            up.start()

        @pl.when(me == n - 1)
        def _():
            dst[pl.ds(DMAX, DMAX), :] = jnp.zeros((DMAX, width), BF16)

    def wait_halo(which, src, dst):
        down, up = halo_copies(which, src, dst)

        @pl.when(me > 0)
        def _():
            up.wait_recv()
            down.wait_send()

        @pl.when(me < n - 1)
        def _():
            down.wait_recv()
            up.wait_send()

    dilation = dil_ref[seg]
    tile = 256

    def selectors():
        t = lax.broadcasted_iota(jnp.int32, (length, length), 0)
        s = lax.broadcasted_iota(jnp.int32, (length, length), 1)
        th = lax.broadcasted_iota(jnp.int32, (length, 2 * DMAX), 0)
        h = lax.broadcasted_iota(jnp.int32, (length, 2 * DMAX), 1)
        one = lambda c: jnp.where(c, 1.0, 0.0).astype(BF16)
        before = (one(s == t - dilation), one((h - DMAX == th - dilation) & (h < DMAX)))
        after = (one(s == t + dilation), one((h - DMAX + length == th + dilation) & (h >= DMAX)))
        return before, after

    def convolve(src, halo, dst, flip):
        before, after = selectors()
        low, high = (2, 0) if flip else (0, 2)

        def body(c, carry):
            cols = pl.ds(pl.multiple_of(c * tile, tile), tile)
            own, edge = src[:, cols], halo[:, cols]
            pick = lambda sel: jnp.dot(sel[0], own, preferred_element_type=F32) + jnp.dot(
                sel[1], edge, preferred_element_type=F32
            )
            value = tap_ref[pl.ds(1, 1), cols] * own.astype(F32)
            value = tap_ref[pl.ds(low, 1), cols] * pick(before) + value
            value = value + tap_ref[pl.ds(high, 1), cols] * pick(after)
            dst[:, cols] = value.astype(dst.dtype)
            return carry

        lax.fori_loop(0, width // tile, body, 0)

    step_rows = 16

    def activate(src, dst):
        def body(i, carry):
            at = pl.ds(pl.multiple_of(i * step_rows, step_rows), step_rows)
            r = src[at, :].astype(F32)
            s = lax.rsqrt(jnp.mean(r * r, axis=-1, keepdims=True) + 1e-06)
            v = r * s
            t = jnp.tanh(ROOT * (v + CUBIC * (v * v * v)))
            dst[at, :] = (0.5 * v * (1.0 + t)).astype(BF16)
            return carry

        lax.fori_loop(0, length // step_rows, body, 0)

    def pull_back(src, grad, store):
        def body(i, carry):
            at = pl.ds(pl.multiple_of(i * step_rows, step_rows), step_rows)
            r = src[at, :].astype(F32)
            s = lax.rsqrt(jnp.mean(r * r, axis=-1, keepdims=True) + 1e-06)
            v = r * s
            vv = v * v
            t = jnp.tanh(ROOT * (v + CUBIC * (vv * v)))
            half = 0.5 * (1.0 + t)
            slope = half + 0.5 * v * (1.0 - t * t) * (ROOT * (1.0 + 3.0 * CUBIC * vv))
            dn = ga[at, :] * slope
            gr = s * (dn - v * jnp.mean(dn * v, axis=-1, keepdims=True))
            store(at, v * half, grad[at, :].astype(F32) + gr)
            return carry

        lax.fori_loop(0, length // step_rows, body, 0)

    def project(grad):
        pb[...] = jnp.dot(grad[...], proj_ref[...], preferred_element_type=F32).astype(BF16)

    def sketch():
        def body(c, carry):
            cols = pl.ds(pl.multiple_of(c * tile, tile), tile)
            value = lax.dot_general(
                pb[...], mixed[:, cols], (((0,), (0,)), ((), ())), preferred_element_type=F32
            ).astype(BF16)
            for k in range(n):
                sk[k, :, cols] = value[k * kr : (k + 1) * kr]
            return carry

        lax.fori_loop(0, width // tile, body, 0)
        for k in range(1, n):
            rs_copy(lax.rem(me + k, n)).start()

    def rs_copy(peer):
        return pltpu.make_async_remote_copy(
            src_ref=sk.at[peer], dst_ref=rs.at[me],
            send_sem=rs_send.at[peer], recv_sem=rs_recv.at[me],
            device_id={"ctx": peer}, device_id_type=MESH,
        )

    def back_product(grad):
        def body(c, carry):
            cols = pl.ds(pl.multiple_of(c * tile, tile), tile)
            gu[:, cols] = lax.dot_general(
                grad[...], wf[cols, :], (((1,), (1,)), ((), ())), preferred_element_type=F32
            ).astype(BF16)
            return carry

        lax.fori_loop(0, width // tile, body, 0)

    def core_copy(index, src, dst):
        return pltpu.make_async_remote_copy(
            src_ref=src, dst_ref=dst, send_sem=c_send.at[index], recv_sem=c_recv.at[index],
            device_id={"segment": 1 - seg}, device_id_type=MESH,
        )

    half = width // 2
    mid_copy = core_copy(0, first, second)
    back_copy = core_copy(1, first, second)
    half_copy = core_copy(2, other, out_ref)

    start_weights()
    wf[pl.ds(pl.multiple_of(me * rows, 16), rows), :] = w_ref[...]

    @pl.when(seg == 0)
    def _():
        activate(x_ref, act)
        start_halo(0, act, halo_a)

    @pl.when(seg == 1)
    def _():
        project(g_ref)

    gather_weights()

    @pl.when(seg == 0)
    def _():
        wait_halo(0, act, halo_a)
        convolve(act, halo_a, mixed, False)

        def body(c, carry):
            cols = pl.ds(pl.multiple_of(c * tile, tile), tile)
            value = jnp.dot(mixed[...], wf[:, cols], preferred_element_type=F32)
            first[:, cols] = (x_ref[:, cols].astype(F32) + value).astype(BF16)
            return carry

        lax.fori_loop(0, width // tile, body, 0)
        mid_copy.start()
        mid_copy.wait_send()
        back_copy.wait_recv()
        project(second)
        sketch()
        back_product(second)
        start_halo(1, gu, halo_g)
        wait_halo(1, gu, halo_g)
        convolve(gu, halo_g, ga, True)

        def store(at, value, grad):
            out_ref[at, :] = grad[:, :half].astype(BF16)
            other[at, :] = grad[:, half:].astype(BF16)

        pull_back(x_ref, second, store)
        half_copy.start()
        half_copy.wait_send()

    @pl.when(seg == 1)
    def _():
        back_product(g_ref)
        start_halo(1, gu, halo_g)
        wait_halo(1, gu, halo_g)
        convolve(gu, halo_g, ga, True)
        mid_copy.wait_recv()

        def store(at, value, grad):
            act[at, :] = value.astype(BF16)
            first[at, :] = grad.astype(BF16)

        pull_back(second, g_ref, store)
        back_copy.start()
        start_halo(0, act, halo_a)
        wait_halo(0, act, halo_a)
        convolve(act, halo_a, mixed, False)
        sketch()
        back_copy.wait_send()
        half_copy.wait_recv()

    total = sk[me].astype(F32)
    for k in range(1, n):
        peer = lax.rem(me + k, n)
        pltpu.make_async_remote_copy(
            src_ref=sk.at[peer], dst_ref=rs.at[peer], send_sem=rs_send.at[peer],
            recv_sem=rs_recv.at[peer], device_id={"ctx": peer}, device_id_type=MESH,
        ).wait_recv()
        total = total + rs[peer].astype(F32)
    dpb[dp] = total.astype(BF16)

    def dp_copy(peer, slot):
        return pltpu.make_async_remote_copy(
            src_ref=dpb.at[slot], dst_ref=dpb.at[slot], send_sem=dp_send.at[peer],
            recv_sem=dp_recv.at[slot], device_id={"dp": peer}, device_id_type=MESH,
        )

    for k in range(1, m):
        dp_copy(lax.rem(dp + k, m), dp).start()
    for k in range(1, m):
        dp_copy(lax.rem(dp + k, m), lax.rem(dp + k, m)).wait_recv()
    merged = dpb[0].astype(F32)
    for k in range(1, m):
        merged = merged + dpb[k].astype(F32)
    sk_ref[...] = merged

    for k in range(1, m):
        dp_copy(lax.rem(dp + k, m), dp).wait_send()
    for k in range(1, n):
        rs_copy(lax.rem(me + k, n)).wait_send()
    for cond, make in pending:

        @pl.when(cond)
        def _():
            make().wait_send()


def shards(inputs, cotangent, weights, tap_weights, projection, dilations):
    n, m = lax.axis_size("ctx"), lax.axis_size("dp")
    length, width = inputs.shape[1:]
    rows = weights.shape[1]
    tests = projection.shape[2]
    kr = tests // n
    vmem = pl.BlockSpec(memory_space=pltpu.VMEM)
    dma = pltpu.SemaphoreType.DMA
    grad, sketches = pl.pallas_call(
        functools.partial(kernel, n, m),
        out_shape=(
            jax.ShapeDtypeStruct((length, width // 2), BF16),
            jax.ShapeDtypeStruct((kr, width), F32),
        ),
        in_specs=[vmem] * 5 + [pl.BlockSpec(memory_space=pltpu.SMEM)],
        out_specs=(vmem, vmem),
        scratch_shapes=[
            pltpu.VMEM((n * rows, width), BF16),
            pltpu.VMEM((length, width), BF16),
            pltpu.VMEM((2 * DMAX, width), BF16),
            pltpu.VMEM((2 * DMAX, width), BF16),
            pltpu.VMEM((length, width), BF16),
            pltpu.VMEM((length, width), BF16),
            pltpu.VMEM((length, width), F32),
            pltpu.VMEM((length, width), BF16),
            pltpu.VMEM((length, width), BF16),
            pltpu.VMEM((length, width // 2), BF16),
            pltpu.VMEM((n, kr, width), BF16),
            pltpu.VMEM((n, kr, width), BF16),
            pltpu.VMEM((m, kr, width), BF16),
            pltpu.VMEM((length, tests), BF16),
            dma((n, 3, 5)),
            dma((n, 3)),
            dma((2, 2)),
            dma((2, 2)),
            dma((3,)),
            dma((3,)),
            dma((n,)),
            dma((n,)),
            dma((m,)),
            dma((m,)),
        ],
        compiler_params=pltpu.CompilerParams(
            collective_id=0, has_side_effects=True, vmem_limit_bytes=48 << 20
        ),
        name="segment",
    )(inputs[0], cotangent[0], weights[0], tap_weights[0], projection[0], dilations)
    return (grad[None], sketches[None])


def solution(mesh):
    in_specs = (
        P("dp", "ctx", None),
        P("dp", "ctx", None),
        P("segment", "ctx", None),
        P("segment", None, None),
        P("segment", None, None),
        P(),
    )
    out_specs = (P("dp", "ctx", "segment"), P("segment", "ctx", None))
    return jax.shard_map(shards, mesh=mesh, in_specs=in_specs, out_specs=out_specs, check_vma=False)
```

time: 246 us -> 105 us (0.43)
  waiting for transfers between devices: 163 us -> 0 us
  Pallas kernels: 0 us -> 96.2 us
  starting transfers between devices: 31.8 us -> 0 us
  matrix products: 16.1 us -> 0 us
  between operations: 15.5 us -> 0.65 us
  other arithmetic: 13.9 us -> 0 us
  local copies, waits for them, and re-layouts: 2.89 us -> 7.27 us
    pallas_call x0 -> x1, Pallas kernels: none -> 96.2 us  [shards(): pl.pallas_call(functools.partial(kernel, n, m), out_shape=(jax.ShapeDtype...]
    all_gather x1 -> x0, waiting for transfers between devices: 62 us -> none  [shards(): full_weights = lax.all_gather(pair_weights, 'ctx', axis=1, tiled=True)]
    reduce_scatter x1 -> x0, waiting for transfers between devices: 53.4 us -> none  [shards(): lax.psum_scatter(local_sketch.astype(jnp.bfloat16), 'ctx', scatter_dimens...]
    ppermute x11 -> x0, starting transfers between devices: 31.5 us -> none  [the longest x4 16.2 us: with_halo(): after = lax.ppermute(leading, axis, down)]
    ppermute x11 -> x0, waiting for transfers between devices: 25.2 us -> none  [the longest x4 18.8 us: with_halo(): after = lax.ppermute(leading, axis, down)]
    psum x1 -> x0, waiting for transfers between devices: 21.7 us -> none  [shards(): merged = lax.psum(summed, 'dp').astype(jnp.float32)]
    dot_general x5 -> x0, matrix products: 16.1 us -> none  [the longest x2 7.09 us: backward(): lax.dot_general(sketched, mixed, (((0,), (0,)), ((), ())), preferred_elem...]
    unnamed x28 -> x13, local copies, waits for them, and re-layouts: 0.64 us -> 7.27 us
  transfers between devices with their start and end apart: 14 -> 0, of which waited for: 10 -> 0; matrix products, arithmetic and copies ran while one was open for 7% -> 0% of each run, Pallas kernels for 0% -> 0%
where the time goes in v1:
time: 105 us; the launch traced here: 104 us
  Pallas kernels  96.2 us (92%)
  local copies, waits for them, and re-layouts  7.27 us (7%)
    pallas_call x1, Pallas kernels, shards(): pl.pallas_call(functools.partial(kernel, n, m), out_shape=(jax.ShapeDtype...  96.2 us
    unnamed x13, local copies, waits for them, and re-layouts  7.27 us

profile of v1, /device:TPU:20, one launch (start us, length us, event | category | flops | bytes accessed | tf_op | source)
XLA Modules:
  0.0 104.1 jit_solution(3408731360469740278)
XLA Ops:
  0.6 0.7 copy.10
  1.4 0.0 copy-start.4
  1.4 0.7 copy-done.4
  2.0 0.0 copy-start
  2.0 1.1 %copy-done = bf16[1,256,1536]{2,1,0:T(8,128)(2,1)S(1)} copy-done((bf16[1,256,1536]{2,1,0:T(8,128)(2,1)S(1)}, bf16[1,256,1536]{2,1,0:T(8,128)(2,1)}, u32[]{:S(2)}) %copy-start) | copy-done | bytes 786456
  3.1 0.0 copy-start.1
  3.2 1.1 %copy-done.1 = bf16[1,256,1536]{2,1,0:T(8,128)(2,1)S(1)} copy-done((bf16[1,256,1536]{2,1,0:T(8,128)(2,1)S(1)}, bf16[1,256,1536]{2,1,0:T(8,128)(2,1)}, u32[]{:S(2)}) %copy-start.1) | copy-done | bytes 786456
  4.3 0.0 copy-start.2
  4.3 1.1 %copy-done.2 = bf16[1,1536,256]{2,1,0:T(8,128)(2,1)S(1)} copy-done((bf16[1,1536,256]{2,1,0:T(8,128)(2,1)S(1)}, bf16[1,1536,256]{2,1,0:T(8,128)(2,1)}, u32[]{:S(2)}) %copy-start.2) | copy-done | bytes 786456
  5.4 0.0 copy-start.3
  5.4 1.1 %copy-done.3 = bf16[1,192,1536]{2,1,0:T(8,128)(2,1)S(1)} copy-done((bf16[1,192,1536]{2,1,0:T(8,128)(2,1)S(1)}, bf16[1,192,1536]{2,1,0:T(8,128)(2,1)}, u32[]{:S(2)}) %copy-start.3) | copy-done | bytes 589848
  6.5 96.2 %segment.1 = (bf16[256,768]{1,0:T(8,128)(2,1)S(1)}, f32[32,1536]{1,0:T(8,128)S(1)}) custom-call(bf16[256,1536]{1,0:T(8,128)(2,1)S(1)} %bitcast.9, bf16[256,1536]{1,0:T(8,128)(2,1)S(1)} %bitcast.10, bf16[192,1536]{1,0:T(8,128)(2,1)S(1)} %bitcast.12, f32[3,1536]{1,0:T(4,128)S(1)} %bitcast.15, bf16[1536,256]{1,0:T(8,128)(2,1)S(1)} %bitcast.11, s32[2]{0:T(128)S(1)} %copy-done.4), custom_call_target="tpu_custom_call" | custom-call | tf_op jit(solution)/shard_map/segment/pallas_call | solution.py:417
  102.7 0.7 copy.13
  103.5 0.7 copy.14
Async XLA Ops:
  1.4 0.7 copy-start.4
  2.0 1.1 %copy-start = (bf16[1,256,1536]{2,1,0:T(8,128)(2,1)S(1)}, bf16[1,256,1536]{2,1,0:T(8,128)(2,1)}, u32[]{:S(2)}) copy-start(bf16[1,256,1536]{2,1,0:T(8,128)(2,1)} %param.6) | copy-start | bytes 2359300
  3.1 1.1 %copy-start.1 = (bf16[1,256,1536]{2,1,0:T(8,128)(2,1)S(1)}, bf16[1,256,1536]{2,1,0:T(8,128)(2,1)}, u32[]{:S(2)}) copy-start(bf16[1,256,1536]{2,1,0:T(8,128)(2,1)} %param.7) | copy-start | bytes 2359300
  4.3 1.1 %copy-start.2 = (bf16[1,1536,256]{2,1,0:T(8,128)(2,1)S(1)}, bf16[1,1536,256]{2,1,0:T(8,128)(2,1)}, u32[]{:S(2)}) copy-start(bf16[1,1536,256]{2,1,0:T(8,128)(2,1)} %param.10) | copy-start | bytes 2359300
  5.4 1.1 %copy-start.3 = (bf16[1,192,1536]{2,1,0:T(8,128)(2,1)S(1)}, bf16[1,192,1536]{2,1,0:T(8,128)(2,1)}, u32[]{:S(2)}) copy-start(bf16[1,192,1536]{2,1,0:T(8,128)(2,1)} %param.8) | copy-start | bytes 1769476

commit v2 on v1

--- a/solution.py
+++ b/solution.py
@@ -23,15 +23,16 @@
 
 
 def kernel(
-    n, m, x_ref, g_ref, w_ref, tap_ref, proj_ref, dil_ref, out_ref, sk_ref,
-    wf, act, halo_a, halo_g, mixed, gu, ga, first, second, other, sk, rs, dpb, pb,
+    n, m, x_hbm, g_hbm, w_hbm, tap_hbm, proj_hbm, dil_hbm, out_ref, sk_ref,
+    io_ref, tap_ref, proj_ref, dil_ref, slope, normed, scale, l_sem, wf, act, halo_a, halo_g, mixed, gu, ga, first, second, other, sk, rs, dpb, pb,
     w_send, w_recv, h_send, h_recv, c_send, c_recv, rs_send, rs_recv, dp_send, dp_recv,
 ):
     me = lax.axis_index("ctx")
     dp = lax.axis_index("dp")
     seg = lax.axis_index("segment")
-    length, width = x_ref.shape
-    rows = w_ref.shape[0]
+    length, width = io_ref.shape
+    rows = w_hbm.shape[1]
+    w_ref = w_hbm.at[0]
     kr = sk.shape[1]
     X = line_width(n)
     Z = n // X
@@ -41,6 +42,25 @@
     parts = 2 if crossing else 1
     pr = rows // 3 if crossing else rows
     q = lax.rem(dp, 2) if crossing else 0
+
+    own_rows = pl.ds(pl.multiple_of(me * rows, 16), rows)
+    loads = [
+        pltpu.make_async_copy(w_ref, wf.at[own_rows], l_sem.at[0]),
+        pltpu.make_async_copy(proj_hbm.at[0], proj_ref, l_sem.at[1]),
+        pltpu.make_async_copy(tap_hbm.at[0], tap_ref, l_sem.at[2]),
+        pltpu.make_async_copy(dil_hbm, dil_ref, l_sem.at[3]),
+    ]
+
+    @pl.when(seg == 0)
+    def _():
+        pltpu.make_async_copy(x_hbm.at[0], io_ref, l_sem.at[4]).start()
+
+    @pl.when(seg == 1)
+    def _():
+        pltpu.make_async_copy(g_hbm.at[0], io_ref, l_sem.at[4]).start()
+
+    for load in loads:
+        load.start()
 
     barrier = pltpu.get_barrier_semaphore()
     for k in range(1, n):
@@ -198,10 +218,10 @@
             down.wait_recv()
             up.wait_send()
 
-    dilation = dil_ref[seg]
     tile = 256
 
     def selectors():
+        dilation = dil_ref[seg]
         t = lax.broadcasted_iota(jnp.int32, (length, length), 0)
         s = lax.broadcasted_iota(jnp.int32, (length, length), 1)
         th = lax.broadcasted_iota(jnp.int32, (length, 2 * DMAX), 0)
@@ -231,19 +251,7 @@
 
     step_rows = 16
 
-    def activate(src, dst):
-        def body(i, carry):
-            at = pl.ds(pl.multiple_of(i * step_rows, step_rows), step_rows)
-            r = src[at, :].astype(F32)
-            s = lax.rsqrt(jnp.mean(r * r, axis=-1, keepdims=True) + 1e-06)
-            v = r * s
-            t = jnp.tanh(ROOT * (v + CUBIC * (v * v * v)))
-            dst[at, :] = (0.5 * v * (1.0 + t)).astype(BF16)
-            return carry
-
-        lax.fori_loop(0, length // step_rows, body, 0)
-
-    def pull_back(src, grad, store):
+    def prepare(src):
         def body(i, carry):
             at = pl.ds(pl.multiple_of(i * step_rows, step_rows), step_rows)
             r = src[at, :].astype(F32)
@@ -252,13 +260,32 @@
             vv = v * v
             t = jnp.tanh(ROOT * (v + CUBIC * (vv * v)))
             half = 0.5 * (1.0 + t)
-            slope = half + 0.5 * v * (1.0 - t * t) * (ROOT * (1.0 + 3.0 * CUBIC * vv))
-            dn = ga[at, :] * slope
-            gr = s * (dn - v * jnp.mean(dn * v, axis=-1, keepdims=True))
-            store(at, v * half, grad[at, :].astype(F32) + gr)
+            act[at, :] = (v * half).astype(BF16)
+            slope[at, :] = half + 0.5 * v * (1.0 - t * t) * (ROOT * (1.0 + 3.0 * CUBIC * vv))
+            normed[at, :] = v
+            scale[at, :] = jnp.broadcast_to(s, (step_rows, 128))
             return carry
 
         lax.fori_loop(0, length // step_rows, body, 0)
+
+    chunk = 64
+
+    def pull_back(grad, store, send):
+        def outer(c, carry):
+            def body(i, carry):
+                at = pl.ds(pl.multiple_of(c * chunk + i * step_rows, step_rows), step_rows)
+                v = normed[at, :]
+                s = scale[at, :][:, :1]
+                dn = ga[at, :] * slope[at, :]
+                gr = s * (dn - v * jnp.mean(dn * v, axis=-1, keepdims=True))
+                store(at, grad[at, :].astype(F32) + gr)
+                return carry
+
+            lax.fori_loop(0, chunk // step_rows, body, 0)
+            send(c).start()
+            return carry
+
+        lax.fori_loop(0, length // chunk, outer, 0)
 
     def project(grad):
         pb[...] = jnp.dot(grad[...], proj_ref[...], preferred_element_type=F32).astype(BF16)
@@ -301,21 +328,33 @@
         )
 
     half = width // 2
-    mid_copy = core_copy(0, first, second)
-    back_copy = core_copy(1, first, second)
-    half_copy = core_copy(2, other, out_ref)
+    tiles, chunks = width // tile, length // chunk
+
+    def mid_copy(c):
+        cols = pl.ds(pl.multiple_of(c * tile, tile), tile)
+        return core_copy(c, first.at[:, cols], second.at[:, cols])
+
+    def back_copy(c):
+        at = pl.ds(pl.multiple_of(c * chunk, chunk), chunk)
+        return core_copy(tiles + c, first.at[at], second.at[at])
+
+    def half_copy(c):
+        at = pl.ds(pl.multiple_of(c * chunk, chunk), chunk)
+        return core_copy(tiles + chunks + c, other.at[at], out_ref.at[at])
 
     start_weights()
-    wf[pl.ds(pl.multiple_of(me * rows, 16), rows), :] = w_ref[...]
+    pltpu.make_async_copy(x_hbm.at[0], io_ref, l_sem.at[4]).wait()
+    for load in loads:
+        load.wait()
 
     @pl.when(seg == 0)
     def _():
-        activate(x_ref, act)
+        prepare(io_ref)
         start_halo(0, act, halo_a)
 
     @pl.when(seg == 1)
     def _():
-        project(g_ref)
+        project(io_ref)
 
     gather_weights()
 
@@ -327,13 +366,15 @@
         def body(c, carry):
             cols = pl.ds(pl.multiple_of(c * tile, tile), tile)
             value = jnp.dot(mixed[...], wf[:, cols], preferred_element_type=F32)
-            first[:, cols] = (x_ref[:, cols].astype(F32) + value).astype(BF16)
+            first[:, cols] = (io_ref[:, cols].astype(F32) + value).astype(BF16)
+            mid_copy(c).start()
             return carry
 
-        lax.fori_loop(0, width // tile, body, 0)
-        mid_copy.start()
-        mid_copy.wait_send()
-        back_copy.wait_recv()
+        lax.fori_loop(0, tiles, body, 0)
+        for c in range(tiles):
+            mid_copy(c).wait_send()
+        for c in range(chunks):
+            back_copy(c).wait_recv()
         project(second)
         sketch()
         back_product(second)
@@ -341,34 +382,36 @@
         wait_halo(1, gu, halo_g)
         convolve(gu, halo_g, ga, True)
 
-        def store(at, value, grad):
+        def store(at, grad):
             out_ref[at, :] = grad[:, :half].astype(BF16)
             other[at, :] = grad[:, half:].astype(BF16)
 
-        pull_back(x_ref, second, store)
-        half_copy.start()
-        half_copy.wait_send()
+        pull_back(second, store, half_copy)
+        for c in range(chunks):
+            half_copy(c).wait_send()
 
     @pl.when(seg == 1)
     def _():
-        back_product(g_ref)
+        back_product(io_ref)
         start_halo(1, gu, halo_g)
+        for c in range(tiles):
+            mid_copy(c).wait_recv()
+        prepare(second)
+        start_halo(0, act, halo_a)
         wait_halo(1, gu, halo_g)
         convolve(gu, halo_g, ga, True)
-        mid_copy.wait_recv()
-
-        def store(at, value, grad):
-            act[at, :] = value.astype(BF16)
+
+        def store(at, grad):
             first[at, :] = grad.astype(BF16)
 
-        pull_back(second, g_ref, store)
-        back_copy.start()
-        start_halo(0, act, halo_a)
+        pull_back(io_ref, store, back_copy)
         wait_halo(0, act, halo_a)
         convolve(act, halo_a, mixed, False)
         sketch()
-        back_copy.wait_send()
-        half_copy.wait_recv()
+        for c in range(chunks):
+            back_copy(c).wait_send()
+        for c in range(chunks):
+            half_copy(c).wait_recv()
 
     total = sk[me].astype(F32)
     for k in range(1, n):
@@ -420,9 +463,17 @@
             jax.ShapeDtypeStruct((length, width // 2), BF16),
             jax.ShapeDtypeStruct((kr, width), F32),
         ),
-        in_specs=[vmem] * 5 + [pl.BlockSpec(memory_space=pltpu.SMEM)],
+        in_specs=[pl.BlockSpec(memory_space=pl.ANY)] * 6,
         out_specs=(vmem, vmem),
         scratch_shapes=[
+            pltpu.VMEM((length, width), BF16),
+            pltpu.VMEM(tap_weights.shape[1:], F32),
+            pltpu.VMEM(projection.shape[1:], BF16),
+            pltpu.SMEM(dilations.shape, jnp.int32),
+            pltpu.VMEM((length, width), F32),
+            pltpu.VMEM((length, width), F32),
+            pltpu.VMEM((length, 128), F32),
+            dma((5,)),
             pltpu.VMEM((n * rows, width), BF16),
             pltpu.VMEM((length, width), BF16),
             pltpu.VMEM((2 * DMAX, width), BF16),
@@ -441,18 +492,18 @@
             dma((n, 3)),
             dma((2, 2)),
             dma((2, 2)),
-            dma((3,)),
-            dma((3,)),
+            dma((width // 256 + 2 * length // 64,)),
+            dma((width // 256 + 2 * length // 64,)),
             dma((n,)),
             dma((n,)),
             dma((m,)),
             dma((m,)),
         ],
         compiler_params=pltpu.CompilerParams(
-            collective_id=0, has_side_effects=True, vmem_limit_bytes=48 << 20
+            collective_id=0, has_side_effects=True, vmem_limit_bytes=60 << 20
         ),
         name="segment",
-    )(inputs[0], cotangent[0], weights[0], tap_weights[0], projection[0], dilations)
+    )(inputs, cotangent, weights, tap_weights, projection, dilations)
     return (grad[None], sketches[None])
 
 

time: 105 us -> 100 us (0.952)
  local copies, waits for them, and re-layouts: 7.27 us -> 3.82 us
    unnamed x13 -> x5, local copies, waits for them, and re-layouts: 7.27 us -> 3.82 us
where the time goes in v2:
time: 100 us
  Pallas kernels  95.6 us (96%)
  local copies, waits for them, and re-layouts  3.82 us (4%)
    pallas_call x1, Pallas kernels, shards(): pl.pallas_call(functools.partial(kernel, n, m), out_shape=(jax.ShapeDtype...  95.6 us
    unnamed x5, local copies, waits for them, and re-layouts  3.82 us

profile of v2, /device:TPU:20, one launch (start us, length us, event | category | flops | bytes accessed | tf_op | source)
XLA Modules:
  0.0 100.1 jit_solution(9111165640261010161)
XLA Ops:
  0.6 1.3 %copy.8.tap_hbm = f32[1,3,1536]{2,1,0:T(4,128)} copy(f32[1,3,1536]{2,0,1:T(1,128)} %param.9) | data formatting | bytes 36864 | tf_op args[3]
  2.0 95.6 %segment.1 = (bf16[256,768]{1,0:T(8,128)(2,1)}, f32[32,1536]{1,0:T(8,128)}) custom-call(bf16[1,256,1536]{2,1,0:T(8,128)(2,1)} %x_hbm.1, bf16[1,256,1536]{2,1,0:T(8,128)(2,1)} %g_hbm.1, bf16[1,192,1536]{2,1,0:T(8,128)(2,1)} %w_hbm.1, f32[1,3,1536]{2,1,0:T(4,128)} %copy.8.tap_hbm, bf16[1,1536,256]{2,1,0:T(8,128)(2,1)} %proj_hbm.1, s32[2]{0:T(128)} %dil_hbm.1), custom_call_target="tpu_custom_call" | custom-call | tf_op jit(solution)/shard_map/segment/pallas_call | solution.py:460
  97.6 0.0 copy-start
  97.6 1.8 %copy.11 = bf16[1,256,768]{2,1,0:T(8,128)(2,1)} copy(bf16[1,256,768]{2,1,0:T(8,128)(2,1)} %bitcast.2) | data formatting | bytes 786432
  99.4 0.0 copy-done
  99.4 0.7 copy.12
Async XLA Ops:
  97.6 1.8 %copy-start = (f32[32,1536]{1,0:T(8,128)S(1)}, f32[32,1536]{1,0:T(8,128)}, u32[]{:S(2)}) copy-start(f32[32,1536]{1,0:T(8,128)} %get-tuple-element.5) | copy-start | bytes 589828

commit v3 on v2

--- a/solution.py
+++ b/solution.py
@@ -23,9 +23,10 @@
 
 
 def kernel(
-    n, m, x_hbm, g_hbm, w_hbm, tap_hbm, proj_hbm, dil_hbm, out_ref, sk_ref,
-    io_ref, tap_ref, proj_ref, dil_ref, slope, normed, scale, l_sem, wf, act, halo_a, halo_g, mixed, gu, ga, first, second, other, sk, rs, dpb, pb,
+    n, m, x_hbm, g_hbm, w_hbm, tap_ref, proj_hbm, dil_hbm, out_ref, sk_ref,
+    io_ref, proj_ref, dil_ref, slope, normed, scale, l_sem, wf, act, halo_a, halo_g, mixed, gu, ga, first, second, other, sk, rs, dpb, pb, ys, yr, keep,
     w_send, w_recv, h_send, h_recv, c_send, c_recv, rs_send, rs_recv, dp_send, dp_recv,
+    y_send, y_recv,
 ):
     me = lax.axis_index("ctx")
     dp = lax.axis_index("dp")
@@ -33,7 +34,7 @@
     length, width = io_ref.shape
     rows = w_hbm.shape[1]
     w_ref = w_hbm.at[0]
-    kr = sk.shape[1]
+    kr = sk.shape[-2]
     X = line_width(n)
     Z = n // X
     z = me // X
@@ -47,7 +48,6 @@
     loads = [
         pltpu.make_async_copy(w_ref, wf.at[own_rows], l_sem.at[0]),
         pltpu.make_async_copy(proj_hbm.at[0], proj_ref, l_sem.at[1]),
-        pltpu.make_async_copy(tap_hbm.at[0], tap_ref, l_sem.at[2]),
         pltpu.make_async_copy(dil_hbm, dil_ref, l_sem.at[3]),
     ]
 
@@ -218,6 +218,8 @@
             down.wait_recv()
             up.wait_send()
 
+    paired = len(sk.shape) == 4
+
     tile = 256
 
     def selectors():
@@ -290,7 +292,86 @@
     def project(grad):
         pb[...] = jnp.dot(grad[...], proj_ref[...], preferred_element_type=F32).astype(BF16)
 
+    pairs = ys.shape[0]
+
+    def y_copy(k):
+        return pltpu.make_async_remote_copy(
+            src_ref=ys.at[k], dst_ref=yr.at[k], send_sem=y_send.at[k], recv_sem=y_recv.at[k],
+            device_id={"dp": 1 - dp}, device_id_type=MESH,
+        )
+
+    def sketch_tile(c):
+        cols = pl.ds(pl.multiple_of(c * tile, tile), tile)
+        return lax.dot_general(
+            pb[...], mixed[:, cols], (((0,), (0,)), ((), ())), preferred_element_type=F32
+        )
+
+    def sketch_pairs():
+        def body(k, carry):
+            value = sketch_tile(2 * k + 1 - dp).astype(BF16)
+            for b in range(n):
+                ys[k, b] = value[b * kr : (b + 1) * kr]
+            y_copy(k).start()
+            return carry
+
+        lax.fori_loop(0, pairs, body, 0)
+
+        def mine(k, carry):
+            value = sketch_tile(2 * k + dp)
+            for b in range(n):
+                keep[k, b] = value[b * kr : (b + 1) * kr]
+            return carry
+
+        lax.fori_loop(0, pairs, mine, 0)
+
+    def c_copy(k, peer, slot):
+        return pltpu.make_async_remote_copy(
+            src_ref=sk.at[k, peer], dst_ref=rs.at[k, slot], send_sem=rs_send.at[k, peer],
+            recv_sem=rs_recv.at[k, slot], device_id={"ctx": peer}, device_id_type=MESH,
+        )
+
+    def spread_pairs():
+        def body(k, carry):
+            y_copy(k).wait_recv()
+            sk[k] = (keep[k] + yr[k].astype(F32)).astype(BF16)
+            for j in range(1, n):
+                c_copy(k, lax.rem(me + j, n), me).start()
+            return carry
+
+        lax.fori_loop(0, pairs, body, 0)
+
+    def d_copy(k, slot):
+        return pltpu.make_async_remote_copy(
+            src_ref=dpb.at[slot, k], dst_ref=dpb.at[slot, k], send_sem=dp_send.at[k],
+            recv_sem=dp_recv.at[k], device_id={"dp": 1 - dp}, device_id_type=MESH,
+        )
+
+    def finish_pairs():
+        def body(k, carry):
+            total = sk[k, me].astype(F32)
+            for j in range(1, n):
+                peer = lax.rem(me + j, n)
+                c_copy(k, peer, peer).wait_recv()
+                total = total + rs[k, peer].astype(F32)
+            dpb[dp, k] = total.astype(BF16)
+            d_copy(k, dp).start()
+            return carry
+
+        lax.fori_loop(0, pairs, body, 0)
+        for k in range(pairs):
+            d_copy(k, 1 - dp).wait_recv()
+            for slot in range(2):
+                c = 2 * k + slot
+                sk_ref[:, c * tile : (c + 1) * tile] = dpb[slot, k].astype(F32)
+        for k in range(pairs):
+            d_copy(k, dp).wait_send()
+            y_copy(k).wait_send()
+            for j in range(1, n):
+                c_copy(k, lax.rem(me + j, n), me).wait_send()
+
     def sketch():
+        if paired:
+            return sketch_pairs()
         def body(c, carry):
             cols = pl.ds(pl.multiple_of(c * tile, tile), tile)
             value = lax.dot_general(
@@ -379,6 +460,8 @@
         sketch()
         back_product(second)
         start_halo(1, gu, halo_g)
+        if paired:
+            spread_pairs()
         wait_halo(1, gu, halo_g)
         convolve(gu, halo_g, ga, True)
 
@@ -408,40 +491,48 @@
         wait_halo(0, act, halo_a)
         convolve(act, halo_a, mixed, False)
         sketch()
+        if paired:
+            spread_pairs()
         for c in range(chunks):
             back_copy(c).wait_send()
         for c in range(chunks):
             half_copy(c).wait_recv()
 
-    total = sk[me].astype(F32)
-    for k in range(1, n):
-        peer = lax.rem(me + k, n)
-        pltpu.make_async_remote_copy(
-            src_ref=sk.at[peer], dst_ref=rs.at[peer], send_sem=rs_send.at[peer],
-            recv_sem=rs_recv.at[peer], device_id={"ctx": peer}, device_id_type=MESH,
-        ).wait_recv()
-        total = total + rs[peer].astype(F32)
-    dpb[dp] = total.astype(BF16)
-
-    def dp_copy(peer, slot):
-        return pltpu.make_async_remote_copy(
-            src_ref=dpb.at[slot], dst_ref=dpb.at[slot], send_sem=dp_send.at[peer],
-            recv_sem=dp_recv.at[slot], device_id={"dp": peer}, device_id_type=MESH,
-        )
-
-    for k in range(1, m):
-        dp_copy(lax.rem(dp + k, m), dp).start()
-    for k in range(1, m):
-        dp_copy(lax.rem(dp + k, m), lax.rem(dp + k, m)).wait_recv()
-    merged = dpb[0].astype(F32)
-    for k in range(1, m):
-        merged = merged + dpb[k].astype(F32)
-    sk_ref[...] = merged
-
-    for k in range(1, m):
-        dp_copy(lax.rem(dp + k, m), dp).wait_send()
-    for k in range(1, n):
-        rs_copy(lax.rem(me + k, n)).wait_send()
+    def finish_direct():
+        total = sk[me].astype(F32)
+        for k in range(1, n):
+            peer = lax.rem(me + k, n)
+            pltpu.make_async_remote_copy(
+                src_ref=sk.at[peer], dst_ref=rs.at[peer], send_sem=rs_send.at[peer],
+                recv_sem=rs_recv.at[peer], device_id={"ctx": peer}, device_id_type=MESH,
+            ).wait_recv()
+            total = total + rs[peer].astype(F32)
+        dpb[dp] = total.astype(BF16)
+
+        def dp_copy(peer, slot):
+            return pltpu.make_async_remote_copy(
+                src_ref=dpb.at[slot], dst_ref=dpb.at[slot], send_sem=dp_send.at[peer],
+                recv_sem=dp_recv.at[slot], device_id={"dp": peer}, device_id_type=MESH,
+            )
+
+        for k in range(1, m):
+            dp_copy(lax.rem(dp + k, m), dp).start()
+        for k in range(1, m):
+            dp_copy(lax.rem(dp + k, m), lax.rem(dp + k, m)).wait_recv()
+        merged = dpb[0].astype(F32)
+        for k in range(1, m):
+            merged = merged + dpb[k].astype(F32)
+        sk_ref[...] = merged
+
+        for k in range(1, m):
+            dp_copy(lax.rem(dp + k, m), dp).wait_send()
+        for k in range(1, n):
+            rs_copy(lax.rem(me + k, n)).wait_send()
+
+    if paired:
+        finish_pairs()
+    else:
+        finish_direct()
     for cond, make in pending:
 
         @pl.when(cond)
@@ -455,6 +546,11 @@
     rows = weights.shape[1]
     tests = projection.shape[2]
     kr = tests // n
+    tile = 256
+    paired = m == 2 and width % (2 * tile) == 0
+    pairs = width // (2 * tile) if paired else 1
+    lead, wide = ((pairs,), tile) if paired else ((), width)
+    hbm = pl.BlockSpec(memory_space=pltpu.HBM)
     vmem = pl.BlockSpec(memory_space=pltpu.VMEM)
     dma = pltpu.SemaphoreType.DMA
     grad, sketches = pl.pallas_call(
@@ -463,11 +559,10 @@
             jax.ShapeDtypeStruct((length, width // 2), BF16),
             jax.ShapeDtypeStruct((kr, width), F32),
         ),
-        in_specs=[pl.BlockSpec(memory_space=pl.ANY)] * 6,
+        in_specs=[hbm, hbm, hbm, vmem, hbm, hbm],
         out_specs=(vmem, vmem),
         scratch_shapes=[
             pltpu.VMEM((length, width), BF16),
-            pltpu.VMEM(tap_weights.shape[1:], F32),
             pltpu.VMEM(projection.shape[1:], BF16),
             pltpu.SMEM(dilations.shape, jnp.int32),
             pltpu.VMEM((length, width), F32),
@@ -484,26 +579,31 @@
             pltpu.VMEM((length, width), BF16),
             pltpu.VMEM((length, width), BF16),
             pltpu.VMEM((length, width // 2), BF16),
-            pltpu.VMEM((n, kr, width), BF16),
-            pltpu.VMEM((n, kr, width), BF16),
-            pltpu.VMEM((m, kr, width), BF16),
+            pltpu.VMEM(lead + (n, kr, wide), BF16),
+            pltpu.VMEM(lead + (n, kr, wide), BF16),
+            pltpu.VMEM((m,) + lead + (kr, wide), BF16),
             pltpu.VMEM((length, tests), BF16),
+            pltpu.VMEM((pairs, n, kr, tile), BF16),
+            pltpu.VMEM((pairs, n, kr, tile), BF16),
+            pltpu.VMEM((pairs, n, kr, tile), F32),
             dma((n, 3, 5)),
             dma((n, 3)),
             dma((2, 2)),
             dma((2, 2)),
             dma((width // 256 + 2 * length // 64,)),
             dma((width // 256 + 2 * length // 64,)),
-            dma((n,)),
-            dma((n,)),
-            dma((m,)),
-            dma((m,)),
+            dma(lead + (n,)),
+            dma(lead + (n,)),
+            dma(lead if paired else (m,)),
+            dma(lead if paired else (m,)),
+            dma((pairs,)),
+            dma((pairs,)),
         ],
         compiler_params=pltpu.CompilerParams(
             collective_id=0, has_side_effects=True, vmem_limit_bytes=60 << 20
         ),
         name="segment",
-    )(inputs, cotangent, weights, tap_weights, projection, dilations)
+    )(inputs, cotangent, weights, tap_weights[0], projection, dilations)
     return (grad[None], sketches[None])
 
 

time: 100 us -> 91.1 us (0.911); the launches traced: 100 us -> 89.6 us
  Pallas kernels: 95.6 us -> 85.1 us
    pallas_call x1, Pallas kernels: 95.6 us -> 85.1 us  [shards(): pl.pallas_call(functools.partial(kernel, n, m), out_shape=(jax.ShapeDtype...]
where the time goes in v3:
time: 91.1 us; the launch traced here: 89.6 us
  Pallas kernels  85.1 us (93%)
  local copies, waits for them, and re-layouts  3.82 us (4%)
    pallas_call x1, Pallas kernels, shards(): pl.pallas_call(functools.partial(kernel, n, m), out_shape=(jax.ShapeDtype...  85.1 us
    unnamed x5, local copies, waits for them, and re-layouts  3.82 us

profile of v3, /device:TPU:20, one launch (start us, length us, event | category | flops | bytes accessed | tf_op | source)
XLA Modules:
  0.0 89.6 jit_solution(9204031343196080420)
XLA Ops:
  0.6 1.3 %copy.10 = f32[1,3,1536]{2,1,0:T(4,128)} copy(f32[1,3,1536]{2,0,1:T(1,128)} %param.9) | data formatting | bytes 36864
  2.0 85.1 %segment.1 = (bf16[256,768]{1,0:T(8,128)(2,1)}, f32[32,1536]{1,0:T(8,128)}) custom-call(bf16[1,256,1536]{2,1,0:T(8,128)(2,1)} %x_hbm.1, bf16[1,256,1536]{2,1,0:T(8,128)(2,1)} %g_hbm.1, bf16[1,192,1536]{2,1,0:T(8,128)(2,1)} %w_hbm.1, f32[3,1536]{1,0:T(4,128)} %bitcast.7, bf16[1,1536,256]{2,1,0:T(8,128)(2,1)} %proj_hbm.1, s32[2]{0:T(128)} %dil_hbm.1), custom_call_target="tpu_custom_call" | custom-call | tf_op jit(solution)/shard_map/segment/pallas_call | solution.py:556
  87.1 0.0 copy-start
  87.1 1.8 %copy.13 = bf16[1,256,768]{2,1,0:T(8,128)(2,1)} copy(bf16[1,256,768]{2,1,0:T(8,128)(2,1)} %bitcast.5) | data formatting | bytes 786432
  88.9 0.0 copy-done
  88.9 0.7 copy.14
Async XLA Ops:
  87.1 1.8 %copy-start = (f32[32,1536]{1,0:T(8,128)S(1)}, f32[32,1536]{1,0:T(8,128)}, u32[]{:S(2)}) copy-start(f32[32,1536]{1,0:T(8,128)} %get-tuple-element.5) | copy-start | bytes 589828

commit v4 on v3

--- a/solution.py
+++ b/solution.py
@@ -62,6 +62,8 @@
     for load in loads:
         load.start()
 
+    order = (2 * q, 1)[:parts]
+
     barrier = pltpu.get_barrier_semaphore()
     for k in range(1, n):
         pl.semaphore_signal(barrier, inc=1, device_id={"ctx": lax.rem(me + k, n)}, device_id_type=MESH)
@@ -128,17 +130,17 @@
     def start_weights():
         for j in range(parts):
             for entry in (
-                sends_z(me, q + j, True, True),
-                sends_z(me, q + j, False, True),
-                sends_x(me, q + j, True, True),
-                sends_x(me, q + j, False, True),
+                sends_z(me, order[j], True, True),
+                sends_z(me, order[j], False, True),
+                sends_x(me, order[j], True, True),
+                sends_x(me, order[j], False, True),
             ):
                 issue(None, entry)
 
     def spread_x(step):
         for t in range(1, X):
             for j in range(parts):
-                part = q + j
+                part = order[j]
                 for sign in (-1, 1):
                     for side in ((0,) if step == 0 else (-1, 1)):
                         zz = z + side * step
@@ -152,10 +154,12 @@
                             issue(guard, sends_x(block, part, sign < 0))
                         cross(guard, block, part)
 
-    def gather_weights():
+    def gather_weights(meanwhile):
+        if Z == 1:
+            meanwhile()
         for step in range(1, Z):
             for j in range(parts):
-                part = q + j
+                part = order[j]
                 for up in (True, False):
                     zz = z - step if up else z + step
                     guard = zz >= 0 if up else zz < Z
@@ -167,6 +171,8 @@
                     issue(guard, sends_x(block, part, False))
                     cross(guard, block, part)
             spread_x(step - 1)
+            if step == 1:
+                meanwhile()
         spread_x(Z - 1)
         if crossing:
             for k in range(1, n):
@@ -437,13 +443,16 @@
     def _():
         project(io_ref)
 
-    gather_weights()
+    def mix_first():
+        @pl.when(seg == 0)
+        def _():
+            wait_halo(0, act, halo_a)
+            convolve(act, halo_a, mixed, False)
+
+    gather_weights(mix_first)
 
     @pl.when(seg == 0)
     def _():
-        wait_halo(0, act, halo_a)
-        convolve(act, halo_a, mixed, False)
-
         def body(c, carry):
             cols = pl.ds(pl.multiple_of(c * tile, tile), tile)
             value = jnp.dot(mixed[...], wf[:, cols], preferred_element_type=F32)

time: 91.1 us -> 86.8 us (0.953)
  Pallas kernels: 85.1 us -> 80.7 us
    pallas_call x1, Pallas kernels: 85.1 us -> 80.7 us  [shards(): pl.pallas_call(functools.partial(kernel, n, m), out_shape=(jax.ShapeDtype...]
where the time goes in v4:
time: 86.8 us; the launch traced here: 85.2 us
  Pallas kernels  80.7 us (93%)
  local copies, waits for them, and re-layouts  3.82 us (4%)
    pallas_call x1, Pallas kernels, shards(): pl.pallas_call(functools.partial(kernel, n, m), out_shape=(jax.ShapeDtype...  80.7 us
    unnamed x5, local copies, waits for them, and re-layouts  3.82 us

profile of v4, /device:TPU:20, one launch (start us, length us, event | category | flops | bytes accessed | tf_op | source)
XLA Modules:
  0.0 85.2 jit_solution(11371453307071528919)
XLA Ops:
  0.6 1.3 %copy.10 = f32[1,3,1536]{2,1,0:T(4,128)} copy(f32[1,3,1536]{2,0,1:T(1,128)} %param.9) | data formatting | bytes 36864
  2.0 80.7 %segment.1 = (bf16[256,768]{1,0:T(8,128)(2,1)}, f32[32,1536]{1,0:T(8,128)}) custom-call(bf16[1,256,1536]{2,1,0:T(8,128)(2,1)} %x_hbm.1, bf16[1,256,1536]{2,1,0:T(8,128)(2,1)} %g_hbm.1, bf16[1,192,1536]{2,1,0:T(8,128)(2,1)} %w_hbm.1, f32[3,1536]{1,0:T(4,128)} %bitcast.7, bf16[1,1536,256]{2,1,0:T(8,128)(2,1)} %proj_hbm.1, s32[2]{0:T(128)} %dil_hbm.1), custom_call_target="tpu_custom_call" | custom-call | tf_op jit(solution)/shard_map/segment/pallas_call | solution.py:565
  82.7 0.0 copy-start
  82.7 1.8 %copy.13 = bf16[1,256,768]{2,1,0:T(8,128)(2,1)} copy(bf16[1,256,768]{2,1,0:T(8,128)(2,1)} %bitcast.5) | data formatting | bytes 786432
  84.5 0.0 copy-done
  84.5 0.7 copy.14
Async XLA Ops:
  82.7 1.8 %copy-start = (f32[32,1536]{1,0:T(8,128)S(1)}, f32[32,1536]{1,0:T(8,128)}, u32[]{:S(2)}) copy-start(f32[32,1536]{1,0:T(8,128)} %get-tuple-element.5) | copy-start | bytes 589828

commit v5 on v4

--- a/solution.py
+++ b/solution.py
@@ -62,6 +62,7 @@
     for load in loads:
         load.start()
 
+    shift = crossing and X == 2 and Z > 1
     order = (2 * q, 1)[:parts]
 
     barrier = pltpu.get_barrier_semaphore()
@@ -152,6 +153,10 @@
                         arrived(guard, block, part)
                         if t < X - 1:
                             issue(guard, sends_x(block, part, sign < 0))
+                        if shift and j == 1:
+                            for up in ((True, False) if step == 0 else (side < 0,)):
+                                end = zz == (0 if up else Z - 1)
+                                issue(jnp.logical_and(guard, end), sends_z(block, part, up))
                         cross(guard, block, part)
 
     def gather_weights(meanwhile):
@@ -167,8 +172,11 @@
                     arrived(guard, block, part)
                     if step < Z - 1:
                         issue(guard, sends_z(block, part, up))
-                    issue(guard, sends_x(block, part, True))
-                    issue(guard, sends_x(block, part, False))
+                    inner = guard
+                    if shift and j == 1:
+                        inner = jnp.logical_and(guard, zz != (0 if up else Z - 1))
+                    issue(inner, sends_x(block, part, True))
+                    issue(inner, sends_x(block, part, False))
                     cross(guard, block, part)
             spread_x(step - 1)
             if step == 1:

time: 86.8 us -> 84.3 us (0.971)
  the two profiles are of different devices: /device:TPU:20 before, /device:TPU:0 now
where the time goes in v5:
time: 84.3 us; the launch traced here: 84 us
  Pallas kernels  79.6 us (94%)
  local copies, waits for them, and re-layouts  3.82 us (5%)
    pallas_call x1, Pallas kernels, shards(): pl.pallas_call(functools.partial(kernel, n, m), out_shape=(jax.ShapeDtype...  79.6 us
    unnamed x5, local copies, waits for them, and re-layouts  3.82 us

profile of v5, /device:TPU:0, one launch (start us, length us, event | category | flops | bytes accessed | tf_op | source)
XLA Modules:
  0.0 84.0 jit_solution(10711697292451974113)
XLA Ops:
  0.6 1.3 %copy.10 = f32[1,3,1536]{2,1,0:T(4,128)} copy(f32[1,3,1536]{2,0,1:T(1,128)} %param.9) | data formatting | bytes 36864
  2.0 79.6 %segment.1 = (bf16[256,768]{1,0:T(8,128)(2,1)}, f32[32,1536]{1,0:T(8,128)}) custom-call(bf16[1,256,1536]{2,1,0:T(8,128)(2,1)} %x_hbm.1, bf16[1,256,1536]{2,1,0:T(8,128)(2,1)} %g_hbm.1, bf16[1,192,1536]{2,1,0:T(8,128)(2,1)} %w_hbm.1, f32[3,1536]{1,0:T(4,128)} %bitcast.7, bf16[1,1536,256]{2,1,0:T(8,128)(2,1)} %proj_hbm.1, s32[2]{0:T(128)} %dil_hbm.1), custom_call_target="tpu_custom_call" | custom-call | tf_op jit(solution)/shard_map/segment/pallas_call | solution.py:573
  81.5 0.0 copy-start
  81.6 1.8 %copy.13 = bf16[1,256,768]{2,1,0:T(8,128)(2,1)} copy(bf16[1,256,768]{2,1,0:T(8,128)(2,1)} %bitcast.5) | data formatting | bytes 786432
  83.4 0.0 copy-done
  83.4 0.7 copy.14
Async XLA Ops:
  81.5 1.8 %copy-start = (f32[32,1536]{1,0:T(8,128)S(1)}, f32[32,1536]{1,0:T(8,128)}, u32[]{:S(2)}) copy-start(f32[32,1536]{1,0:T(8,128)} %get-tuple-element.5) | copy-start | bytes 589828
